TPU v7x, 32 devices: a whole 2x2x4 slice. The times are simulated.
32 devices in a mesh: req: 4 (over z), seq: 8 (over y, x, core).
Axes of the slice: x: 2, y: 2, z: 4, core: 2. Of those that a mesh axis runs over, the one named last changes fastest.
Arguments:
- hidden_in: bfloat16 [4, 32, 4, 2048], P(None, 'req', None, 'seq'), may hold values from -30 to 30
- cache_lens: int32 [32], P('req'), may hold values from 1 to 4092, as said below
- page_table: int32 [32, 32], P('req'), may hold values from -1 to 55, as said below
- key_cache: bfloat16 [224, 128, 1024], P(('req', 'seq')), may hold values from -250 to 250
- value_cache: bfloat16 [224, 128, 1024], P(('req', 'seq')), may hold values from -4 to 4
- norm_attn: float32 [8192], replicated, may hold values from 0.1 to 1.9
- w_qkv: bfloat16 [8192, 10240], P(None, 'seq'), may hold values from -0.0625 to 0.0625
- b_qkv: bfloat16 [10240], P('seq'), may hold values from -3 to 3
- w_out: bfloat16 [8192, 4, 2048], P(None, None, 'seq'), may hold values from -0.25 to 0.25
- norm_mlp: float32 [8192], replicated, may hold values from 0.1 to 1.9
- w_gate: bfloat16 [8192, 29568], P('req', 'seq'), may hold values from -0.0625 to 0.0625
- w_up: bfloat16 [8192, 29568], P('req', 'seq'), may hold values from -0.0625 to 0.0625
- w_down: bfloat16 [29568, 8192], P('seq', 'req'), may hold values from -0.03125 to 0.03125
Outputs:
- hidden_out: bfloat16 [4, 32, 4, 2048], P(None, 'req', None, 'seq')
- key_cache_out: bfloat16 [224, 128, 1024], P(('req', 'seq'))
- value_cache_out: bfloat16 [224, 128, 1024], P(('req', 'seq'))
Inputs may be any that keep to these rules, and one draw needn't show every extreme that they name: `cache_lens`: in each group of 8 requests exactly one holds 4092 tokens and one holds 380; every other one holds at most 380. For request r and logical page j below ceil((cache_lens[r]+4)/128), page_table[r, j] is a slot of the group's 56 page slots (slot s*7+p is the p-th slot of seq index s); no slot is named twice within a group; all other entries are -1.
All inputs are finite; a program needn't handle non-finite values.
Results may differ from a plain program's by a relative error of at most 0.012.
The roundings to bfloat16 on the way count: a program that leaves them out, or rounds other values in their place, can miss the bound.
Values may be sent and summed in bfloat16 or wider, within the bound.
A program may use at most 320 MiB of HBM per device.

v0:
```python
import math
import jax
import jax.numpy as jnp
from jax import lax
from jax.sharding import PartitionSpec as P

D = 8192
H = 64
KV = 8
HD = 128
STEPS = 4
EPSILON = 1e-06
THETA = 1000000.0
NEGATIVE = -1e30


def rotate(heads, position):
    half = heads.shape[-1] // 2
    freq = THETA ** (-(jnp.arange(half, dtype=jnp.float32) * 2.0 / heads.shape[-1]))
    angle = position.astype(jnp.float32)[:, None, None] * freq[None, None, :]
    cosine = jnp.cos(angle)
    sine = jnp.sin(angle)
    first = heads[..., :half]
    second = heads[..., half:]
    return jnp.concatenate(
        [first * cosine - second * sine, second * cosine + first * sine], axis=-1
    )


def on_device(
    hidden_in,
    cache_lens,
    page_table,
    key_cache,
    value_cache,
    norm_attn,
    w_qkv,
    b_qkv,
    w_out,
    norm_mlp,
    w_gate,
    w_up,
    w_down,
):
    steps, requests, blocks, pieces = hidden_in.shape
    rows = steps * requests
    slots, per_page, _ = key_cache.shape
    group = H // KV
    quarter = D // blocks
    seq = quarter // pieces
    scale = 1.0 / math.sqrt(HD)
    slot_ids = lax.axis_index("seq") * slots + jnp.arange(slots, dtype=jnp.int32)
    matches = page_table[:, :, None] == slot_ids[None, None, :]
    live = jnp.any(matches, axis=(0, 1))
    owner = jnp.sum(
        jnp.where(matches, jnp.arange(requests, dtype=jnp.int32)[:, None, None], 0), axis=(0, 1)
    )
    logical = jnp.sum(
        jnp.where(matches, jnp.arange(page_table.shape[1], dtype=jnp.int32)[None, :, None], 0),
        axis=(0, 1),
    )
    owned = jnp.logical_and(
        jnp.arange(requests, dtype=jnp.int32)[None, :] == owner[:, None], live[:, None]
    )
    slot_length = jnp.sum(jnp.where(owned, cache_lens[None, :], 0), axis=1)
    positions = logical[:, None] * per_page + jnp.arange(per_page, dtype=jnp.int32)[None, :]
    flat = lax.all_gather(hidden_in, "seq", axis=3, tiled=True).reshape(rows, D).astype(jnp.float32)
    normed = (
        flat * lax.rsqrt(jnp.mean(flat * flat, axis=1, keepdims=True) + EPSILON) * norm_attn
    ).astype(jnp.bfloat16)
    columns = (
        jnp.dot(normed, w_qkv, preferred_element_type=jnp.float32) + b_qkv.astype(jnp.float32)
    ).astype(jnp.bfloat16)
    projected = lax.all_gather(columns, "seq", axis=1, tiled=True)
    position = (jnp.arange(steps, dtype=jnp.int32)[:, None] + cache_lens[None, :]).reshape(rows)
    rotated = rotate(
        projected[:, : (H + KV) * HD].reshape(rows, H + KV, HD).astype(jnp.float32), position
    ).astype(jnp.bfloat16)
    queries = rotated[:, :H].reshape(steps, requests, KV, group, HD)
    new_keys = rotated[:, H:].reshape(steps, requests, KV * HD)
    new_values = projected[:, (H + KV) * HD :].reshape(steps, requests, KV * HD)
    slot_keys = jnp.take(new_keys, owner, axis=1)
    slot_values = jnp.take(new_values, owner, axis=1)
    for step in range(steps):
        write_here = jnp.logical_and(live[:, None], positions == (slot_length + step)[:, None])[
            :, :, None
        ]
        key_cache = jnp.where(write_here, slot_keys[step][:, None, :], key_cache)
        value_cache = jnp.where(write_here, slot_values[step][:, None, :], value_cache)
    slot_queries = jnp.take(queries, owner, axis=1)
    keys_view = key_cache.reshape(slots, per_page, KV, HD)
    values_view = value_cache.reshape(slots, per_page, KV, HD)
    scores = (
        jnp.einsum("tjkgd,jpkd->jktgp", slot_queries, keys_view, preferred_element_type=jnp.float32)
        * scale
    )
    last = slot_length[:, None] + jnp.arange(steps, dtype=jnp.int32)[None, :]
    valid = jnp.logical_and(live[:, None, None], positions[:, None, :] <= last[:, :, None])[
        :, None, :, None, :
    ]
    masked = jnp.where(valid, scores, NEGATIVE)
    page_max = jnp.max(masked, axis=4)
    weights = jnp.where(valid, jnp.exp(masked - page_max[..., None]), 0.0).astype(jnp.bfloat16)
    page_sum = jnp.sum(weights.astype(jnp.float32), axis=4)
    page_acc = jnp.einsum(
        "jktgp,jpkd->jktgd", weights, values_view, preferred_element_type=jnp.float32
    )
    spread = owned[:, :, None, None, None]
    candidates = jnp.where(spread, page_max[:, None], NEGATIVE)
    top = jnp.max(candidates, axis=0)
    factor = jnp.where(spread, jnp.exp(candidates - top[None]), 0.0)
    total = jnp.sum(factor * page_sum[:, None], axis=0)
    summed = jnp.sum(factor[..., None] * page_acc[:, None], axis=0)

    def by_head(value):
        value = jnp.moveaxis(value, 0, 3)
        value = jnp.swapaxes(value, 1, 2)
        return value.reshape((seq, H // seq, rows) + value.shape[4:])

    packed = jnp.concatenate(
        [
            by_head(summed).reshape(seq, -1),
            by_head(top).reshape(seq, -1),
            by_head(total).reshape(seq, -1),
        ],
        axis=1,
    )
    packed = lax.all_to_all(packed, "seq", split_axis=0, concat_axis=0, tiled=True)
    count = H // seq * rows
    part_acc = packed[:, : count * HD].reshape(seq, count, HD)
    part_top = packed[:, count * HD : count * (HD + 1)]
    part_sum = packed[:, count * (HD + 1) :]
    best = jnp.max(part_top, axis=0)
    share = jnp.exp(part_top - best[None])
    denominator = jnp.sum(share * part_sum, axis=0)
    numerator = jnp.sum(share[..., None] * part_acc, axis=0)
    heads = (numerator / denominator[:, None]).astype(jnp.bfloat16)
    heads = jnp.swapaxes(heads.reshape(H // seq, rows, HD), 0, 1).reshape(rows, -1)
    attended = lax.all_gather(heads, "seq", axis=1, tiled=True)
    branch_out = jnp.dot(
        attended, w_out.reshape(H * HD, blocks * pieces), preferred_element_type=jnp.float32
    ).reshape(rows, blocks, pieces)
    current = hidden_in.reshape(rows, blocks, pieces).astype(jnp.float32)
    middle = (current + branch_out).astype(jnp.bfloat16)
    rows_mid = lax.all_gather(middle, "seq", axis=2, tiled=True).astype(jnp.float32)
    inverse = lax.rsqrt(jnp.mean(rows_mid * rows_mid, axis=(1, 2), keepdims=True) + EPSILON)
    normed_mid = (rows_mid * inverse * norm_mlp.reshape(blocks, quarter)).astype(jnp.bfloat16)
    mine = lax.all_to_all(normed_mid, "req", split_axis=1, concat_axis=0, tiled=True).reshape(
        -1, quarter
    )
    gate_part = jnp.dot(mine, w_gate, preferred_element_type=jnp.float32).astype(jnp.bfloat16)
    up_part = jnp.dot(mine, w_up, preferred_element_type=jnp.float32).astype(jnp.bfloat16)
    gate_sum = lax.psum_scatter(gate_part, "req", scatter_dimension=0, tiled=True)
    up_sum = lax.psum_scatter(up_part, "req", scatter_dimension=0, tiled=True)
    hidden_part = (jax.nn.silu(gate_sum.astype(jnp.float32)) * up_sum.astype(jnp.float32)).astype(
        jnp.bfloat16
    )
    hidden = lax.all_gather(hidden_part, "req", axis=0, tiled=True)
    down = jnp.dot(hidden, w_down, preferred_element_type=jnp.float32)
    sums = lax.psum_scatter(
        down.reshape(down.shape[0], 1, quarter).astype(jnp.bfloat16),
        "seq",
        scatter_dimension=2,
        tiled=True,
    ).astype(jnp.float32)
    back = lax.all_to_all(sums, "req", split_axis=0, concat_axis=1, tiled=True)
    output = (middle.astype(jnp.float32) + back).astype(jnp.bfloat16)
    return (output.reshape(hidden_in.shape), key_cache, value_cache)


def solution(mesh):
    in_specs = (
        P(None, "req", None, "seq"),
        P("req"),
        P("req", None),
        P(("req", "seq"), None, None),
        P(("req", "seq"), None, None),
        P(),
        P(None, "seq"),
        P("seq"),
        P(None, None, "seq"),
        P(),
        P("req", "seq"),
        P("req", "seq"),
        P("seq", "req"),
    )
    out_specs = (
        P(None, "req", None, "seq"),
        P(("req", "seq"), None, None),
        P(("req", "seq"), None, None),
    )
    return jax.shard_map(
        on_device, mesh=mesh, in_specs=in_specs, out_specs=out_specs, check_vma=False
    )
```

profile of v0, /device:TPU:0, one launch (start us, length us, event | category | flops | bytes accessed | tf_op | source)
XLA Modules:
  0.0 303.2 jit_solution(10138137191504181131)
XLA Ops:
  9.3 11.7 %all_gather.15 = bf16[4,8,4,2048]{3,2,1,0:T(4,128)(2,1)S(1)} all-gather(bf16[4,8,4,256]{3,2,1,0:T(4,128)(2,1)} %param.15), channel_id=1, replica_groups=mesh['req'=4,'seq'=8] {'seq'}, dimensions={3}, use_global_device_ids=true | all-gather | bytes 589824 | tf_op jit(solution)/shard_map/all_gather | solution.py:67
  22.2 9.0 %fusion.1 = bf16[32,1280]{1,0:T(8,128)(2,1)S(1)} fusion(bf16[8192,1280]{1,0:T(8,128)(2,1)} %param.21, f32[32,8192]{1,0:T(8,128)S(1)} %bitcast.124, f32[8192]{0:T(1024)S(1)} %copy-done.5, f32[32]{0:T(128)S(1)} %rsqrt.20, f32[1280]{0:T(1024)S(1)} %convert_element_type.96), kind=kOutput, calls=%fused_computation.9 | convolution fusion | flops 671956992 | bytes 22140032 | tf_op jit(solution)/shard_map/dot_general | solution.py:72
  31.2 10.3 %all_gather.16 = bf16[32,10240]{1,0:T(8,128)(2,1)S(1)} all-gather(bf16[32,1280]{1,0:T(8,128)(2,1)S(1)} %fusion.1), channel_id=1, replica_groups=mesh['req'=4,'seq'=8] {'seq'}, dimensions={1}, use_global_device_ids=true | all-gather | bytes 737280 | tf_op jit(solution)/shard_map/all_gather | solution.py:74
  45.7 2.8 select_select_fusion
  49.7 1.4 bitcast_bitcast_fusion.1
  51.8 2.7 fusion.48
  59.1 2.3 multiply_reduce_fusion
  62.7 2.1 copy.101
  64.8 3.6 %all-to-all-start = ((f32[8,1,33280]{2,1,0:T(1,128)}), f32[8,1,33280]{2,1,0:T(1,128)S(1)}, u32[]{:S(2)}, u32[]{:S(2)}) async-start(f32[8,1,33280]{2,1,0:T(1,128)} %copy.101), calls=%async_computation | async-start | bytes 2129920 | tf_op jit(solution)/shard_map/all_to_all | solution.py:128
  68.6 16.8 %copy.129 = bf16[1024,8,4,256]{3,1,2,0:T(8,128)(2,1)} copy(bf16[1024,8,4,256]{3,2,1,0:T(4,128)(2,1)} %bitcast.118) | data formatting | bytes 33554432
  85.4 20.9 %copy.104 = bf16[1024,8192]{1,0:T(8,128)(2,1)} copy(bf16[1024,8192]{0,1:T(8,128)(2,1)} %bitcast.117) | data formatting | bytes 33554432 | tf_op jit(solution)/shard_map/dot_general | solution.py:140
  107.2 10.0 %all_gather.17 = bf16[32,8192]{1,0:T(8,128)(2,1)S(1)} all-gather(bf16[32,1024]{1,0:T(8,128)(2,1)S(1)} %copy_bitcast_fusion.2), channel_id=1, replica_groups=mesh['req'=4,'seq'=8] {'seq'}, dimensions={1}, use_global_device_ids=true | all-gather | bytes 589824 | tf_op jit(solution)/shard_map/all_gather | solution.py:139
  117.2 10.8 %fusion.12 = bf16[32,4,256]{2,0,1:T(8,128)(2,1)S(1)} fusion(bf16[4,256,8192]{2,1,0:T(8,128)(2,1)} %bitcast.116, bf16[32,8192]{1,0:T(8,128)(2,1)S(1)} %all_gather.17, f32[4,8,4,256]{3,2,1,0:T(4,128)S(1)} %convert_element_type.118), kind=kOutput, calls=%fused_computation.30 | convolution fusion | flops 536936448 | bytes 17498112 | tf_op jit(solution)/shard_map/dot_general | solution.py:140
  128.0 11.2 %all_gather.18 = bf16[32,4,2048]{2,0,1:T(8,128)(2,1)S(1)} all-gather(bf16[32,4,256]{2,0,1:T(8,128)(2,1)S(1)} %fusion.12), channel_id=1, replica_groups=mesh['req'=4,'seq'=8] {'seq'}, dimensions={2}, use_global_device_ids=true | all-gather | bytes 589824 | tf_op jit(solution)/shard_map/all_gather | solution.py:145
  139.7 19.7 %all_to_all.45 = bf16[32,4,2048]{2,0,1:T(8,128)(2,1)S(1)} all-to-all(bf16[32,4,2048]{2,0,1:T(8,128)(2,1)S(1)} %fusion.15), channel_id=1, replica_groups=mesh['req'=4,'seq'=8] {'req'}, dimensions={1} | all-to-all | bytes 1048576 | tf_op jit(solution)/shard_map/all_to_all | solution.py:148
  159.4 11.3 %convolution_convert_fusion = bf16[128,3696]{1,0:T(8,128)(2,1)} fusion(bf16[128,2048]{1,0:T(8,128)(2,1)S(1)} %bitcast.125, bf16[2048,3696]{0,1:T(8,128)(2,1)} %param.26), kind=kOutput, calls=%fused_computation.4 | convolution fusion | flops 1938241536 | bytes 16609280 | tf_op jit(solution)/shard_map/dot_general | solution.py:152
  171.0 11.5 %convolution_convert_fusion.1 = bf16[128,3696]{1,0:T(8,128)(2,1)} fusion(bf16[128,2048]{1,0:T(8,128)(2,1)S(1)} %bitcast.126, bf16[2048,3696]{0,1:T(8,128)(2,1)} %param.25), kind=kOutput, calls=%fused_computation.5 | convolution fusion | flops 1938241536 | bytes 16609280 | tf_op jit(solution)/shard_map/dot_general | solution.py:151
  182.6 12.0 %reduce-scatter.6.cloned.1.call-done = bf16[32,3696]{1,0:T(8,128)(2,1)} async-done(((bf16[128,3696]{1,0:T(8,128)(2,1)}), bf16[32,3696]{1,0:T(8,128)(2,1)}) %reduce-scatter.6.cloned.1.call-update) | async-done | bytes 236560 | tf_op jit(solution)/shard_map/reduce_scatter | solution.py:154
  194.6 26.8 %reduce-scatter.4.cloned.1.call-done = bf16[32,3696]{1,0:T(8,128)(2,1)} async-done(((bf16[128,3696]{1,0:T(8,128)(2,1)}), bf16[32,3696]{1,0:T(8,128)(2,1)}) %reduce-scatter.4.cloned.1.call-update) | async-done | bytes 236560 | tf_op jit(solution)/shard_map/reduce_scatter | solution.py:153
  221.4 1.2 fusion.28
  222.6 19.6 %all_gather.19 = bf16[128,3696]{1,0:T(8,128)(2,1)S(1)} all-gather(bf16[32,3696]{1,0:T(8,128)(2,1)S(1)} %fusion.28), channel_id=1, replica_groups=mesh['req'=4,'seq'=8] {'req'}, dimensions={0}, use_global_device_ids=true | all-gather | bytes 1182720 | tf_op jit(solution)/shard_map/all_gather | solution.py:158
  242.3 8.5 %fusion = bf16[128,1,2048]{2,0,1:T(8,128)(2,1)} fusion(bf16[128,3696]{1,0:T(8,128)(2,1)S(1)} %all_gather.19, bf16[3696,2048]{1,0:T(8,128)(2,1)} %param.27), kind=kOutput, calls=%fused_computation.7 | convolution fusion | flops 1938030592 | bytes 16609280 | tf_op jit(solution)/shard_map/dot_general | solution.py:159
  250.8 33.8 %reduce-scatter.8.cloned.1.call-done = bf16[128,1,256]{2,0,1:T(8,128)(2,1)} async-done(((bf16[128,1,2048]{2,0,1:T(8,128)(2,1)}), bf16[128,1,256]{2,0,1:T(8,128)(2,1)}) %reduce-scatter.8.cloned.1.call-update) | async-done | bytes 65552 | tf_op jit(solution)/shard_map/reduce_scatter | solution.py:160
  285.6 10.3 %all_to_all.46 = f32[128,1,256]{2,1,0:T(1,128)S(1)} all-to-all(f32[128,1,256]{2,1,0:T(1,128)S(1)} %copy.105), channel_id=1, replica_groups=mesh['req'=4,'seq'=8] {'req'}, dimensions={0} | all-to-all | bytes 262144 | tf_op jit(solution)/shard_map/all_to_all | solution.py:166
  (105 shorter events, 18.6 us)
Async XLA Ops:
  21.0 1.2 copy-start.7
  21.0 1.2 copy-start.5
  41.5 0.7 copy-start.8
  48.5 1.2 copy-start.1
  48.5 7.9 %copy-start = (bf16[7,128,1024]{2,1,0:T(8,128)(2,1)}, bf16[7,128,1024]{2,1,0:T(8,128)(2,1)S(1)}, u32[]{:S(2)}) copy-start(bf16[7,128,1024]{2,1,0:T(8,128)(2,1)S(1)} %get-tuple-element.41) | copy-start | bytes 5505028
  54.5 1.2 copy-start.2
  57.0 1.2 copy-start.3
  62.7 5.9 %copy-start.4 = (bf16[4,8,4,256]{3,2,1,0:T(4,128)(2,1)S(1)}, bf16[4,8,4,256]{3,2,1,0:T(4,128)(2,1)}, u32[]{:S(2)}) copy-start(bf16[4,8,4,256]{3,2,1,0:T(4,128)(2,1)} %param.15) | copy-start | bytes 196612
  64.8 41.6 %all-to-all-start = ((f32[8,1,33280]{2,1,0:T(1,128)}), f32[8,1,33280]{2,1,0:T(1,128)S(1)}, u32[]{:S(2)}, u32[]{:S(2)}) async-start(f32[8,1,33280]{2,1,0:T(1,128)} %copy.101), calls=%async_computation | async-start | bytes 2129920 | tf_op jit(solution)/shard_map/all_to_all | solution.py:128
  68.3 126.3 %reduce-scatter.6.cloned.1.call-start = ((), (), s32[]{:S(2)}) async-start(), calls=%async_computation.7 | async-start | bytes 1187840 | tf_op jit(solution)/shard_map/reduce_scatter | solution.py:154
  85.4 20.9 %copy-start.6 = (f32[8192]{0:T(1024)S(1)}, f32[8192]{0:T(1024)}, u32[]{:S(2)}) copy-start(f32[8192]{0:T(1024)} %param.24) | copy-start | bytes 98308
  170.7 50.7 %reduce-scatter.4.cloned.1.call-start = ((), (), s32[]{:S(2)}) async-start(), calls=%async_computation.6 | async-start | bytes 1187840 | tf_op jit(solution)/shard_map/reduce_scatter | solution.py:153
  182.5 102.1 %reduce-scatter.8.cloned.1.call-start = ((), (), s32[]{:S(2)}) async-start(), calls=%async_computation.8 | async-start | bytes 589824 | tf_op jit(solution)/shard_map/reduce_scatter | solution.py:160
Sparse Core Ops, SparseCore 0:
  170.8 23.7 reduce-scatter.5
  197.0 24.3 reduce-scatter.3
  250.9 33.6 reduce-scatter.7
where the time goes:
time: 305 us; the launch traced here: 303 us
  blocking collectives  92.9 us (30%)
  waiting for transfers between devices  72.7 us (24%)
  matrix products  54.4 us (18%)
  local copies, waits for them, and re-layouts  51.7 us (17%)
  between operations  14.2 us (5%)
  other arithmetic  13 us (4%)
  starting transfers between devices  4.16 us (1%)
    reduce_scatter x1, waiting for transfers between devices, on_device(): lax.psum_scatter(down.reshape(down.shape[0], 1, quarter).astype(jnp.bfloa...  33.8 us
    reduce_scatter x1, waiting for transfers between devices, on_device(): lax.psum_scatter(gate_part, 'req', scatter_dimension=0, tiled=True)  26.8 us
    unnamed x35, local copies, waits for them, and re-layouts  22.2 us
    dot_general x1, local copies, waits for them, and re-layouts, on_device(): jnp.dot(attended, w_out.reshape(H * HD, blocks * pieces), preferred_eleme...  20.9 us
    all_to_all x1, blocking collectives, on_device(): lax.all_to_all(normed_mid, 'req', split_axis=1, concat_axis=0, tiled=True)  19.7 us
    all_gather x1, blocking collectives, on_device(): hidden = lax.all_gather(hidden_part, 'req', axis=0, tiled=True)  19.6 us
    reduce_scatter x1, waiting for transfers between devices, on_device(): up_sum = lax.psum_scatter(up_part, 'req', scatter_dimension=0, tiled=True)  12 us
    all_gather x1, blocking collectives, on_device(): lax.all_gather(hidden_in, 'seq', axis=3, tiled=True).reshape(rows, D)  11.7 us
  transfers between devices with their start and end apart: 4, of which 3 were waited for; matrix products, arithmetic and copies ran while one was open for 16% of the time, Pallas kernels for 0%

commit v1 on v0

--- a/solution.py
+++ b/solution.py
@@ -71,7 +71,12 @@
     columns = (
         jnp.dot(normed, w_qkv, preferred_element_type=jnp.float32) + b_qkv.astype(jnp.float32)
     ).astype(jnp.bfloat16)
-    projected = lax.all_gather(columns, "seq", axis=1, tiled=True)
+    ring = [columns]
+    for hop in range(7):
+        ring.append(lax.ppermute(ring[-1], "seq", [(dev, (dev + 1) % 8) for dev in range(8)]))
+    projected = jnp.roll(
+        jnp.concatenate(ring[::-1], axis=1), (lax.axis_index("seq") + 1) * ring[0].shape[1], axis=1
+    )
     position = (jnp.arange(steps, dtype=jnp.int32)[:, None] + cache_lens[None, :]).reshape(rows)
     rotated = rotate(
         projected[:, : (H + KV) * HD].reshape(rows, H + KV, HD).astype(jnp.float32), position

time: 305 us -> 325 us (1.066)
  waiting for transfers between devices: 72.7 us -> 104 us
  blocking collectives: 92.9 us -> 82.6 us
    ppermute x0 -> x7, waiting for transfers between devices: none -> 31.4 us  [on_device(): lax.ppermute(ring[-1], 'seq', [(dev, (dev + 1) % 8) for dev in range(8)])]
    all_gather x1 -> x0, blocking collectives: 10.3 us -> none  [on_device(): projected = lax.all_gather(columns, 'seq', axis=1, tiled=True)]
    unnamed x35 -> x52, local copies, waits for them, and re-layouts: 22.2 us -> 22 us
  transfers between devices with their start and end apart: 4 -> 11, of which waited for: 3 -> 10; matrix products, arithmetic and copies ran while one was open for 16% -> 16% of each run, Pallas kernels for 0% -> 0%
where the time goes in v1:
time: 325 us; the launch traced here: 324 us
  waiting for transfers between devices  104 us (32%)
  blocking collectives  82.6 us (25%)
  matrix products  54.4 us (17%)
  local copies, waits for them, and re-layouts  51.6 us (16%)
  between operations  14.4 us (4%)
  other arithmetic  11.8 us (4%)
  starting transfers between devices  4.73 us (1%)
    reduce_scatter x1, waiting for transfers between devices, on_device(): lax.psum_scatter(down.reshape(down.shape[0], 1, quarter).astype(jnp.bfloa...  33.9 us
    ppermute x7, waiting for transfers between devices, on_device(): lax.ppermute(ring[-1], 'seq', [(dev, (dev + 1) % 8) for dev in range(8)])  31.4 us
    reduce_scatter x1, waiting for transfers between devices, on_device(): lax.psum_scatter(gate_part, 'req', scatter_dimension=0, tiled=True)  26.8 us
    unnamed x52, local copies, waits for them, and re-layouts  22 us
    dot_general x1, local copies, waits for them, and re-layouts, on_device(): jnp.dot(attended, w_out.reshape(H * HD, blocks * pieces), preferred_eleme...  20.9 us
    all_to_all x1, blocking collectives, on_device(): lax.all_to_all(normed_mid, 'req', split_axis=1, concat_axis=0, tiled=True)  19.7 us
    all_gather x1, blocking collectives, on_device(): hidden = lax.all_gather(hidden_part, 'req', axis=0, tiled=True)  19.7 us
    reduce_scatter x1, waiting for transfers between devices, on_device(): up_sum = lax.psum_scatter(up_part, 'req', scatter_dimension=0, tiled=True)  12 us
  transfers between devices with their start and end apart: 11, of which 10 were waited for; matrix products, arithmetic and copies ran while one was open for 16% of the time, Pallas kernels for 0%

profile of v1, /device:TPU:0, one launch (start us, length us, event | category | flops | bytes accessed | tf_op | source)
XLA Modules:
  0.0 323.7 jit_solution(18245377537429550827)
XLA Ops:
  7.2 11.7 %all_gather.12 = bf16[4,8,4,2048]{3,2,1,0:T(4,128)(2,1)S(1)} all-gather(bf16[4,8,4,256]{3,2,1,0:T(4,128)(2,1)} %param.15), channel_id=1, replica_groups=mesh['req'=4,'seq'=8] {'seq'}, dimensions={3}, use_global_device_ids=true | all-gather | bytes 589824 | tf_op jit(solution)/shard_map/all_gather | solution.py:67
  20.2 9.0 %fusion.1 = bf16[32,1280]{1,0:T(8,128)(2,1)S(1)} fusion(bf16[8192,1280]{1,0:T(8,128)(2,1)} %param.21, f32[32,8192]{1,0:T(8,128)S(1)} %bitcast.124, f32[8192]{0:T(1024)S(1)} %copy-done.5, f32[32]{0:T(128)S(1)} %rsqrt.20, f32[1280]{0:T(1024)S(1)} %convert_element_type.96), kind=kOutput, calls=%fused_computation.9 | convolution fusion | flops 671956992 | bytes 22140032 | tf_op jit(solution)/shard_map/dot_general | solution.py:72
  31.0 3.0 collective-permute-done
  34.0 4.7 %collective-permute-done.1 = bf16[32,1280]{1,0:T(8,128)(2,1)S(1)} collective-permute-done((bf16[32,1280]{1,0:T(8,128)(2,1)S(1)}, bf16[32,1280]{1,0:T(8,128)(2,1)S(1)}, u32[]{:S(2)}, u32[]{:S(2)}) %collective-permute-start.1) | collective-permute-done | bytes 81952 | tf_op jit(solution)/shard_map/ppermute | solution.py:76
  38.8 4.7 %collective-permute-done.2 = bf16[32,1280]{1,0:T(8,128)(2,1)S(1)} collective-permute-done((bf16[32,1280]{1,0:T(8,128)(2,1)S(1)}, bf16[32,1280]{1,0:T(8,128)(2,1)S(1)}, u32[]{:S(2)}, u32[]{:S(2)}) %collective-permute-start.2) | collective-permute-done | bytes 81952 | tf_op jit(solution)/shard_map/ppermute | solution.py:76
  43.5 4.8 %collective-permute-done.3 = bf16[32,1280]{1,0:T(8,128)(2,1)S(1)} collective-permute-done((bf16[32,1280]{1,0:T(8,128)(2,1)S(1)}, bf16[32,1280]{1,0:T(8,128)(2,1)S(1)}, u32[]{:S(2)}, u32[]{:S(2)}) %collective-permute-start.3) | collective-permute-done | bytes 81952 | tf_op jit(solution)/shard_map/ppermute | solution.py:76
  48.3 4.8 %collective-permute-done.4 = bf16[32,1280]{1,0:T(8,128)(2,1)S(1)} collective-permute-done((bf16[32,1280]{1,0:T(8,128)(2,1)S(1)}, bf16[32,1280]{1,0:T(8,128)(2,1)S(1)}, u32[]{:S(2)}, u32[]{:S(2)}) %collective-permute-start.4) | collective-permute-done | bytes 81952 | tf_op jit(solution)/shard_map/ppermute | solution.py:76
  53.0 4.8 %collective-permute-done.5 = bf16[32,1280]{1,0:T(8,128)(2,1)S(1)} collective-permute-done((bf16[32,1280]{1,0:T(8,128)(2,1)S(1)}, bf16[32,1280]{1,0:T(8,128)(2,1)S(1)}, u32[]{:S(2)}, u32[]{:S(2)}) %collective-permute-start.5) | collective-permute-done | bytes 81952 | tf_op jit(solution)/shard_map/ppermute | solution.py:76
  57.8 4.8 %collective-permute-done.6 = bf16[32,1280]{1,0:T(8,128)(2,1)S(1)} collective-permute-done((bf16[32,1280]{1,0:T(8,128)(2,1)S(1)}, bf16[32,1280]{1,0:T(8,128)(2,1)S(1)}, u32[]{:S(2)}, u32[]{:S(2)}) %collective-permute-start.6) | collective-permute-done | bytes 81952 | tf_op jit(solution)/shard_map/ppermute | solution.py:76
  85.2 3.7 %all-to-all-start = ((f32[8,1,33280]{2,1,0:T(1,128)}), f32[8,1,33280]{2,1,0:T(1,128)S(1)}, u32[]{:S(2)}, u32[]{:S(2)}) async-start(f32[8,1,33280]{2,1,0:T(1,128)} %copy.101), calls=%async_computation | async-start | bytes 2129920 | tf_op jit(solution)/shard_map/all_to_all | solution.py:133
  89.2 16.8 %copy.129 = bf16[1024,8,4,256]{3,1,2,0:T(8,128)(2,1)} copy(bf16[1024,8,4,256]{3,2,1,0:T(4,128)(2,1)} %bitcast.118) | data formatting | bytes 33554432
  105.9 20.9 %copy.104 = bf16[1024,8192]{1,0:T(8,128)(2,1)} copy(bf16[1024,8192]{0,1:T(8,128)(2,1)} %bitcast.117) | data formatting | bytes 33554432 | tf_op jit(solution)/shard_map/dot_general | solution.py:145
  127.7 10.0 %all_gather.13 = bf16[32,8192]{1,0:T(8,128)(2,1)S(1)} all-gather(bf16[32,1024]{1,0:T(8,128)(2,1)S(1)} %copy_bitcast_fusion.2), channel_id=1, replica_groups=mesh['req'=4,'seq'=8] {'seq'}, dimensions={1}, use_global_device_ids=true | all-gather | bytes 589824 | tf_op jit(solution)/shard_map/all_gather | solution.py:144
  137.7 10.8 %fusion.12 = bf16[32,4,256]{2,0,1:T(8,128)(2,1)S(1)} fusion(bf16[4,256,8192]{2,1,0:T(8,128)(2,1)} %bitcast.116, bf16[32,8192]{1,0:T(8,128)(2,1)S(1)} %all_gather.13, f32[4,8,4,256]{3,2,1,0:T(4,128)S(1)} %convert_element_type.118), kind=kOutput, calls=%fused_computation.30 | convolution fusion | flops 536936448 | bytes 17498112 | tf_op jit(solution)/shard_map/dot_general | solution.py:145
  148.6 11.2 %all_gather.14 = bf16[32,4,2048]{2,0,1:T(8,128)(2,1)S(1)} all-gather(bf16[32,4,256]{2,0,1:T(8,128)(2,1)S(1)} %fusion.12), channel_id=1, replica_groups=mesh['req'=4,'seq'=8] {'seq'}, dimensions={2}, use_global_device_ids=true | all-gather | bytes 589824 | tf_op jit(solution)/shard_map/all_gather | solution.py:150
  160.2 19.7 %all_to_all.45 = bf16[32,4,2048]{2,0,1:T(8,128)(2,1)S(1)} all-to-all(bf16[32,4,2048]{2,0,1:T(8,128)(2,1)S(1)} %fusion.15), channel_id=1, replica_groups=mesh['req'=4,'seq'=8] {'req'}, dimensions={1} | all-to-all | bytes 1048576 | tf_op jit(solution)/shard_map/all_to_all | solution.py:153
  179.9 11.3 %convolution_convert_fusion = bf16[128,3696]{1,0:T(8,128)(2,1)} fusion(bf16[128,2048]{1,0:T(8,128)(2,1)S(1)} %bitcast.125, bf16[2048,3696]{0,1:T(8,128)(2,1)} %param.26), kind=kOutput, calls=%fused_computation.4 | convolution fusion | flops 1938241536 | bytes 16609280 | tf_op jit(solution)/shard_map/dot_general | solution.py:157
  191.5 11.5 %convolution_convert_fusion.1 = bf16[128,3696]{1,0:T(8,128)(2,1)} fusion(bf16[128,2048]{1,0:T(8,128)(2,1)S(1)} %bitcast.126, bf16[2048,3696]{0,1:T(8,128)(2,1)} %param.25), kind=kOutput, calls=%fused_computation.5 | convolution fusion | flops 1938241536 | bytes 16609280 | tf_op jit(solution)/shard_map/dot_general | solution.py:156
  203.1 12.0 %reduce-scatter.6.cloned.1.call-done = bf16[32,3696]{1,0:T(8,128)(2,1)} async-done(((bf16[128,3696]{1,0:T(8,128)(2,1)}), bf16[32,3696]{1,0:T(8,128)(2,1)}) %reduce-scatter.6.cloned.1.call-update) | async-done | bytes 236560 | tf_op jit(solution)/shard_map/reduce_scatter | solution.py:159
  215.1 26.8 %reduce-scatter.4.cloned.1.call-done = bf16[32,3696]{1,0:T(8,128)(2,1)} async-done(((bf16[128,3696]{1,0:T(8,128)(2,1)}), bf16[32,3696]{1,0:T(8,128)(2,1)}) %reduce-scatter.4.cloned.1.call-update) | async-done | bytes 236560 | tf_op jit(solution)/shard_map/reduce_scatter | solution.py:158
  243.1 19.7 %all_gather.15 = bf16[128,3696]{1,0:T(8,128)(2,1)S(1)} all-gather(bf16[32,3696]{1,0:T(8,128)(2,1)S(1)} %fusion.28), channel_id=1, replica_groups=mesh['req'=4,'seq'=8] {'req'}, dimensions={0}, use_global_device_ids=true | all-gather | bytes 1182720 | tf_op jit(solution)/shard_map/all_gather | solution.py:163
  262.8 8.5 %fusion = bf16[128,1,2048]{2,0,1:T(8,128)(2,1)} fusion(bf16[128,3696]{1,0:T(8,128)(2,1)S(1)} %all_gather.15, bf16[3696,2048]{1,0:T(8,128)(2,1)} %param.27), kind=kOutput, calls=%fused_computation.7 | convolution fusion | flops 1938030592 | bytes 16609280 | tf_op jit(solution)/shard_map/dot_general | solution.py:164
  271.3 33.9 %reduce-scatter.8.cloned.1.call-done = bf16[128,1,256]{2,0,1:T(8,128)(2,1)} async-done(((bf16[128,1,2048]{2,0,1:T(8,128)(2,1)}), bf16[128,1,256]{2,0,1:T(8,128)(2,1)}) %reduce-scatter.8.cloned.1.call-update) | async-done | bytes 65552 | tf_op jit(solution)/shard_map/reduce_scatter | solution.py:165
  306.1 10.3 %all_to_all.46 = f32[128,1,256]{2,1,0:T(1,128)S(1)} all-to-all(f32[128,1,256]{2,1,0:T(1,128)S(1)} %copy.105), channel_id=1, replica_groups=mesh['req'=4,'seq'=8] {'req'}, dimensions={0} | all-to-all | bytes 262144 | tf_op jit(solution)/shard_map/all_to_all | solution.py:171
  (137 shorter events, 30.1 us)
Async XLA Ops:
  19.0 1.1 copy-start.8
  19.0 1.1 copy-start.5
  20.1 9.4 %copy-start.7 = (s32[8,32]{1,0:T(8,128)S(1)}, s32[8,32]{1,0:T(8,128)}, u32[]{:S(2)}) copy-start(s32[8,32]{1,0:T(8,128)} %param.17) | copy-start | bytes 3076
  20.2 10.1 %copy-start.9 = (s32[8]{0:T(128)S(1)}, s32[8]{0:T(128)}, u32[]{:S(2)}) copy-start(s32[8]{0:T(128)} %param.16) | copy-start | bytes 100
  29.1 4.8 %collective-permute-start = (bf16[32,1280]{1,0:T(8,128)(2,1)S(1)}, bf16[32,1280]{1,0:T(8,128)(2,1)S(1)}, u32[]{:S(2)}, u32[]{:S(2)}) collective-permute-start(bf16[32,1280]{1,0:T(8,128)(2,1)S(1)} %fusion.1), channel_id=1, source_target_pairs={{0,1},{1,2},{2,3},{3,4},{4,5},{5,6},{6,7},{7,0},{8,9},{9,10},{10,1... | collective-permute-start | bytes 245768 | tf_op jit(solution)/shard_map/ppermute | solution.py:76
  34.0 4.8 %collective-permute-start.1 = (bf16[32,1280]{1,0:T(8,128)(2,1)S(1)}, bf16[32,1280]{1,0:T(8,128)(2,1)S(1)}, u32[]{:S(2)}, u32[]{:S(2)}) collective-permute-start(bf16[32,1280]{1,0:T(8,128)(2,1)S(1)} %collective-permute-done), channel_id=1, source_target_pairs={{0,1},{1,2},{2,3},{3,4},{4,5},{5,6},{6,7},{7,0},{8,9},{9,10},{10,1... | collective-permute-start | bytes 245768 | tf_op jit(solution)/shard_map/ppermute | solution.py:76
  38.7 4.8 %collective-permute-start.2 = (bf16[32,1280]{1,0:T(8,128)(2,1)S(1)}, bf16[32,1280]{1,0:T(8,128)(2,1)S(1)}, u32[]{:S(2)}, u32[]{:S(2)}) collective-permute-start(bf16[32,1280]{1,0:T(8,128)(2,1)S(1)} %collective-permute-done.1), channel_id=1, source_target_pairs={{0,1},{1,2},{2,3},{3,4},{4,5},{5,6},{6,7},{7,0},{8,9},{9,10},{10,1... | collective-permute-start | bytes 245768 | tf_op jit(solution)/shard_map/ppermute | solution.py:76
  43.5 4.8 %collective-permute-start.3 = (bf16[32,1280]{1,0:T(8,128)(2,1)S(1)}, bf16[32,1280]{1,0:T(8,128)(2,1)S(1)}, u32[]{:S(2)}, u32[]{:S(2)}) collective-permute-start(bf16[32,1280]{1,0:T(8,128)(2,1)S(1)} %collective-permute-done.2), channel_id=1, source_target_pairs={{0,1},{1,2},{2,3},{3,4},{4,5},{5,6},{6,7},{7,0},{8,9},{9,10},{10,1... | collective-permute-start | bytes 245768 | tf_op jit(solution)/shard_map/ppermute | solution.py:76
  48.2 4.8 %collective-permute-start.4 = (bf16[32,1280]{1,0:T(8,128)(2,1)S(1)}, bf16[32,1280]{1,0:T(8,128)(2,1)S(1)}, u32[]{:S(2)}, u32[]{:S(2)}) collective-permute-start(bf16[32,1280]{1,0:T(8,128)(2,1)S(1)} %collective-permute-done.3), channel_id=1, source_target_pairs={{0,1},{1,2},{2,3},{3,4},{4,5},{5,6},{6,7},{7,0},{8,9},{9,10},{10,1... | collective-permute-start | bytes 245768 | tf_op jit(solution)/shard_map/ppermute | solution.py:76
  53.0 4.8 %collective-permute-start.5 = (bf16[32,1280]{1,0:T(8,128)(2,1)S(1)}, bf16[32,1280]{1,0:T(8,128)(2,1)S(1)}, u32[]{:S(2)}, u32[]{:S(2)}) collective-permute-start(bf16[32,1280]{1,0:T(8,128)(2,1)S(1)} %collective-permute-done.4), channel_id=1, source_target_pairs={{0,1},{1,2},{2,3},{3,4},{4,5},{5,6},{6,7},{7,0},{8,9},{9,10},{10,1... | collective-permute-start | bytes 245768 | tf_op jit(solution)/shard_map/ppermute | solution.py:76
  57.8 4.8 %collective-permute-start.6 = (bf16[32,1280]{1,0:T(8,128)(2,1)S(1)}, bf16[32,1280]{1,0:T(8,128)(2,1)S(1)}, u32[]{:S(2)}, u32[]{:S(2)}) collective-permute-start(bf16[32,1280]{1,0:T(8,128)(2,1)S(1)} %collective-permute-done.5), channel_id=1, source_target_pairs={{0,1},{1,2},{2,3},{3,4},{4,5},{5,6},{6,7},{7,0},{8,9},{9,10},{10,1... | collective-permute-start | bytes 245768 | tf_op jit(solution)/shard_map/ppermute | solution.py:76
  69.0 1.2 copy-start.1
  69.0 7.8 %copy-start = (bf16[7,128,1024]{2,1,0:T(8,128)(2,1)}, bf16[7,128,1024]{2,1,0:T(8,128)(2,1)S(1)}, u32[]{:S(2)}) copy-start(bf16[7,128,1024]{2,1,0:T(8,128)(2,1)S(1)} %get-tuple-element.41) | copy-start | bytes 5505028
  74.9 1.2 copy-start.2
  77.4 1.2 copy-start.3
  85.2 4.0 %copy-start.4 = (bf16[4,8,4,256]{3,2,1,0:T(4,128)(2,1)S(1)}, bf16[4,8,4,256]{3,2,1,0:T(4,128)(2,1)}, u32[]{:S(2)}) copy-start(bf16[4,8,4,256]{3,2,1,0:T(4,128)(2,1)} %param.15) | copy-start | bytes 196612
  85.2 41.7 %all-to-all-start = ((f32[8,1,33280]{2,1,0:T(1,128)}), f32[8,1,33280]{2,1,0:T(1,128)S(1)}, u32[]{:S(2)}, u32[]{:S(2)}) async-start(f32[8,1,33280]{2,1,0:T(1,128)} %copy.101), calls=%async_computation | async-start | bytes 2129920 | tf_op jit(solution)/shard_map/all_to_all | solution.py:133
  88.9 126.3 %reduce-scatter.6.cloned.1.call-start = ((), (), s32[]{:S(2)}) async-start(), calls=%async_computation.7 | async-start | bytes 1187840 | tf_op jit(solution)/shard_map/reduce_scatter | solution.py:159
  105.9 20.9 %copy-start.6 = (f32[8192]{0:T(1024)S(1)}, f32[8192]{0:T(1024)}, u32[]{:S(2)}) copy-start(f32[8192]{0:T(1024)} %param.24) | copy-start | bytes 98308
  191.2 50.7 %reduce-scatter.4.cloned.1.call-start = ((), (), s32[]{:S(2)}) async-start(), calls=%async_computation.6 | async-start | bytes 1187840 | tf_op jit(solution)/shard_map/reduce_scatter | solution.py:158
  203.1 102.1 %reduce-scatter.8.cloned.1.call-start = ((), (), s32[]{:S(2)}) async-start(), calls=%async_computation.8 | async-start | bytes 589824 | tf_op jit(solution)/shard_map/reduce_scatter | solution.py:165
Sparse Core Ops, SparseCore 0:
  191.3 23.7 reduce-scatter.5
  217.5 24.3 reduce-scatter.3
  271.4 33.6 reduce-scatter.7
